TPU v7x, 32 devices: a whole 2x2x4 slice. The times are simulated.
32 devices in a mesh: shard: 8 (over z, x), seq: 4 (over y, core).
Axes of the slice: x: 2, y: 2, z: 4, core: 2. Of those that a mesh axis runs over, the one named last changes fastest.
Arguments:
- clips: bfloat16 [8, 1568, 1024], P('shard', 'seq'), may hold values from -6 to 6
- clip_mask: int32 [8], P('shard'), may hold values 0 or 1
- norm1_gain: float32 [1024], P(('shard', 'seq')), may hold values from 0.1 to 1.9
- norm1_shift: float32 [1024], P(('shard', 'seq')), may hold values from -3 to 3
- query_weight: float32 [1024, 1024], P(('shard', 'seq')), may hold values from -0.1875 to 0.1875
- query_bias: float32 [1024], P(('shard', 'seq')), may hold values from -3 to 3
- key_weight: float32 [1024, 1024], P(('shard', 'seq')), may hold values from -0.1875 to 0.1875
- value_weight: float32 [1024, 1024], P(('shard', 'seq')), may hold values from -0.1875 to 0.1875
- value_bias: float32 [1024], P(('shard', 'seq')), may hold values from -0.3 to 0.3
- out_weight: float32 [1024, 1024], P(('shard', 'seq')), may hold values from -4 to 4
- out_bias: float32 [1024], P(('shard', 'seq')), may hold values from -1.2 to 1.2
- norm2_gain: float32 [1024], P(('shard', 'seq')), may hold values from 0.1 to 1.9
- norm2_shift: float32 [1024], P(('shard', 'seq')), may hold values from -3 to 3
- fc1_weight: float32 [1024, 4096], P(('shard', 'seq')), may hold values from -0.1875 to 0.1875
- fc1_bias: float32 [4096], P(('shard', 'seq')), may hold values from -3 to 3
- fc2_weight: float32 [4096, 1024], P(('shard', 'seq')), may hold values from -0.09375 to 0.09375
- fc2_bias: float32 [1024], P(('shard', 'seq')), may hold values from -1.2 to 1.2
- cotangent: bfloat16 [8, 1568, 1024], P('shard', 'seq'), may hold values from -6 to 6
Outputs:
- layer_out: bfloat16 [8, 1568, 1024], P('shard', 'seq')
- grad_clips: bfloat16 [8, 1568, 1024], P('shard', 'seq')
- grad_norm1_gain: float32 [1024], P(('shard', 'seq'))
- grad_norm1_shift: float32 [1024], P(('shard', 'seq'))
- grad_query_weight: float32 [1024, 1024], P(('shard', 'seq'))
- grad_query_bias: float32 [1024], P(('shard', 'seq'))
- grad_key_weight: float32 [1024, 1024], P(('shard', 'seq'))
- grad_value_weight: float32 [1024, 1024], P(('shard', 'seq'))
- grad_value_bias: float32 [1024], P(('shard', 'seq'))
- grad_out_weight: float32 [1024, 1024], P(('shard', 'seq'))
- grad_out_bias: float32 [1024], P(('shard', 'seq'))
- grad_norm2_gain: float32 [1024], P(('shard', 'seq'))
- grad_norm2_shift: float32 [1024], P(('shard', 'seq'))
- grad_fc1_weight: float32 [1024, 4096], P(('shard', 'seq'))
- grad_fc1_bias: float32 [4096], P(('shard', 'seq'))
- grad_fc2_weight: float32 [4096, 1024], P(('shard', 'seq'))
- grad_fc2_bias: float32 [1024], P(('shard', 'seq'))
All inputs are finite; a program needn't handle non-finite values. No bound on the sum of `clip_mask` on one device may be relied on, other than what follows from the above.
Results may differ from a plain program's by a relative error of at most 0.012.
The roundings to bfloat16 on the way count: a program that leaves them out, or rounds other values in their place, can miss the bound.
Values may be sent and summed in bfloat16 or wider, within the bound.
A program may use at most 192 MiB of HBM per device.

v0:
```python
import jax
import jax.numpy as jnp
from jax import lax
from jax.sharding import PartitionSpec as P

HEAD_DIM = 64


EPSILON = 1e-06


def for_sending(value):
    return jax.tree.map(lambda a: a.astype(jnp.bfloat16) if a.dtype == jnp.float32 else a, value)


def matmul(left, right):
    return jnp.dot(left, right, preferred_element_type=jnp.float32)


def matmul_right_t(left, right):
    return lax.dot_general(
        left, right, (((1,), (1,)), ((), ())), preferred_element_type=jnp.float32
    )


def matmul_left_t(left, right):
    return lax.dot_general(
        left, right, (((0,), (0,)), ((), ())), preferred_element_type=jnp.float32
    )


def gelu_exact(values):
    return jax.nn.gelu(values, approximate=False)


def normalize(values):
    average = jnp.mean(values, -1, keepdims=True)
    centred = values - average
    variance = jnp.mean(centred * centred, -1, keepdims=True)
    inverse = lax.rsqrt(variance + EPSILON)
    return (centred * inverse, inverse)


def norm_back(grad_normed, normed, inverse, gain):
    grad_gain = jnp.sum(grad_normed * normed, 0)
    grad_shift = jnp.sum(grad_normed, 0)
    scaled = grad_normed * gain
    plain_mean = jnp.mean(scaled, -1, keepdims=True)
    cross_mean = jnp.mean(scaled * normed, -1, keepdims=True)
    return (grad_gain, grad_shift, inverse * (scaled - plain_mean - normed * cross_mean))


def attend_clip(inputs):
    query, keys, values = inputs
    length = query.shape[0]
    heads = query.shape[1] // HEAD_DIM
    scale = HEAD_DIM ** (-0.5)
    query = query.reshape(length, heads, HEAD_DIM)
    keys = keys.reshape(length, heads, HEAD_DIM)
    values = values.reshape(length, heads, HEAD_DIM)
    half = length // 2
    outputs = []
    totals = []
    for block in range(2):
        rows_query = query[block * half : (block + 1) * half]
        scores = (
            jnp.einsum("qhd,khd->hqk", rows_query, keys, preferred_element_type=jnp.float32) * scale
        )
        row_max = jnp.max(scores, -1, keepdims=True)
        raised = jnp.exp(scores - row_max)
        summed = jnp.sum(raised, -1, keepdims=True)
        probs = (raised / summed).astype(jnp.bfloat16)
        mixed = jnp.einsum("hqk,khd->qhd", probs, values, preferred_element_type=jnp.float32)
        outputs.append(mixed.astype(jnp.bfloat16))
        totals.append((row_max + jnp.log(summed))[..., 0])
    joined = jnp.concatenate(outputs, 0).reshape(length, heads * HEAD_DIM)
    return (joined, jnp.concatenate(totals, 1))


def attend_back(inputs):
    query, keys, values, totals, grad_out = inputs
    length = query.shape[0]
    heads = query.shape[1] // HEAD_DIM
    scale = HEAD_DIM ** (-0.5)
    query = query.reshape(length, heads, HEAD_DIM)
    keys = keys.reshape(length, heads, HEAD_DIM)
    values = values.reshape(length, heads, HEAD_DIM)
    grad_out = grad_out.reshape(length, heads, HEAD_DIM)
    half = length // 2
    grad_keys = jnp.zeros((length, heads, HEAD_DIM), jnp.float32)
    grad_values = jnp.zeros((length, heads, HEAD_DIM), jnp.float32)
    query_parts = []
    for block in range(2):
        rows_query = query[block * half : (block + 1) * half]
        rows_grad = grad_out[block * half : (block + 1) * half]
        scores = (
            jnp.einsum("qhd,khd->hqk", rows_query, keys, preferred_element_type=jnp.float32) * scale
        )
        probs = jnp.exp(scores - totals[:, block * half : (block + 1) * half, None])
        grad_probs = jnp.einsum(
            "qhd,khd->hqk", rows_grad, values, preferred_element_type=jnp.float32
        )
        weighted = jnp.sum(probs * grad_probs, -1, keepdims=True)
        grad_scores = (probs * (grad_probs - weighted)).astype(jnp.bfloat16)
        part = (
            jnp.einsum("hqk,khd->qhd", grad_scores, keys, preferred_element_type=jnp.float32)
            * scale
        )
        query_parts.append(part.astype(jnp.bfloat16))
        grad_keys = (
            grad_keys
            + jnp.einsum(
                "hqk,qhd->khd", grad_scores, rows_query, preferred_element_type=jnp.float32
            )
            * scale
        )
        grad_values = grad_values + jnp.einsum(
            "hqk,qhd->khd",
            probs.astype(jnp.bfloat16),
            rows_grad,
            preferred_element_type=jnp.float32,
        )
    width = heads * HEAD_DIM
    grad_query = jnp.concatenate(query_parts, 0).reshape(length, width)
    return (
        grad_query,
        grad_keys.astype(jnp.bfloat16).reshape(length, width),
        grad_values.astype(jnp.bfloat16).reshape(length, width),
    )


def fetch_first(masters):
    return (
        lax.all_gather(masters[0].astype(jnp.bfloat16), ("shard", "seq"), axis=0, tiled=True),
        lax.all_gather(masters[1].astype(jnp.bfloat16), ("shard", "seq"), axis=0, tiled=True),
        lax.all_gather(masters[2].astype(jnp.bfloat16), ("shard", "seq"), axis=0, tiled=True),
        lax.all_gather(masters[3].astype(jnp.bfloat16), ("shard", "seq"), axis=0, tiled=True),
        lax.all_gather(masters[4].astype(jnp.bfloat16), ("shard", "seq"), axis=0, tiled=True),
        lax.all_gather(masters[5].astype(jnp.bfloat16), ("shard", "seq"), axis=0, tiled=True),
        lax.all_gather(masters[6].astype(jnp.bfloat16), ("shard", "seq"), axis=0, tiled=True),
        lax.all_gather(masters[7].astype(jnp.bfloat16), ("shard", "seq"), axis=0, tiled=True),
        lax.all_gather(masters[8].astype(jnp.bfloat16), ("shard", "seq"), axis=0, tiled=True),
        lax.all_gather(masters[9].astype(jnp.bfloat16), ("shard", "seq"), axis=0, tiled=True),
        lax.all_gather(masters[10].astype(jnp.bfloat16), ("shard", "seq"), axis=0, tiled=True),
        lax.all_gather(masters[11].astype(jnp.bfloat16), ("shard", "seq"), axis=0, tiled=True),
        lax.all_gather(masters[12].astype(jnp.bfloat16), ("shard", "seq"), axis=0, tiled=True),
        lax.all_gather(masters[13].astype(jnp.bfloat16), ("shard", "seq"), axis=0, tiled=True),
        lax.all_gather(masters[14].astype(jnp.bfloat16), ("shard", "seq"), axis=0, tiled=True),
    )


def on_device(
    clips,
    clip_mask,
    norm1_gain,
    norm1_shift,
    query_weight,
    query_bias,
    key_weight,
    value_weight,
    value_bias,
    out_weight,
    out_bias,
    norm2_gain,
    norm2_shift,
    fc1_weight,
    fc1_bias,
    fc2_weight,
    fc2_bias,
    cotangent,
):
    masters = (
        norm1_gain,
        norm1_shift,
        query_weight,
        query_bias,
        key_weight,
        value_weight,
        value_bias,
        out_weight,
        out_bias,
        norm2_gain,
        norm2_shift,
        fc1_weight,
        fc1_bias,
        fc2_weight,
        fc2_bias,
    )
    fetched = fetch_first(masters)
    (
        gain_first,
        shift_first,
        query_matrix,
        query_offset,
        key_matrix,
        value_matrix,
        value_offset,
        output_matrix,
        output_offset,
        gain_second,
        shift_second,
        expand_matrix,
        expand_offset,
        reduce_matrix,
        reduce_offset,
    ) = fetched
    count, local_length, width = clips.shape
    tokens = count * local_length
    inputs = clips.astype(jnp.float32).reshape(tokens, width)
    normed_one, inverse_one = normalize(inputs)
    hidden_one = (
        normed_one * gain_first.astype(jnp.float32) + shift_first.astype(jnp.float32)
    ).astype(jnp.bfloat16)
    query = (matmul(hidden_one, query_matrix) + query_offset.astype(jnp.float32)).astype(
        jnp.bfloat16
    )
    keys = matmul(hidden_one, key_matrix).astype(jnp.bfloat16)
    values = (matmul(hidden_one, value_matrix) + value_offset.astype(jnp.float32)).astype(
        jnp.bfloat16
    )
    query_heads, key_heads, value_heads = (
        lax.all_to_all(
            query.reshape(count, local_length, width),
            "seq",
            split_axis=2,
            concat_axis=1,
            tiled=True,
        ),
        lax.all_to_all(
            keys.reshape(count, local_length, width), "seq", split_axis=2, concat_axis=1, tiled=True
        ),
        lax.all_to_all(
            values.reshape(count, local_length, width),
            "seq",
            split_axis=2,
            concat_axis=1,
            tiled=True,
        ),
    )
    mixed_heads, totals = lax.map(attend_clip, (query_heads, key_heads, value_heads))
    mixed = (
        lax.all_to_all(for_sending(mixed_heads), "seq", split_axis=1, concat_axis=2, tiled=True)
        .astype(mixed_heads.dtype)
        .reshape(tokens, width)
    )
    middle = inputs + matmul(mixed, output_matrix) + output_offset.astype(jnp.float32)
    normed_two, inverse_two = normalize(middle)
    hidden_two = (
        normed_two * gain_second.astype(jnp.float32) + shift_second.astype(jnp.float32)
    ).astype(jnp.bfloat16)
    inner = matmul(hidden_two, expand_matrix) + expand_offset.astype(jnp.float32)
    active_float, gelu_pullback = jax.vjp(gelu_exact, inner)
    active = active_float.astype(jnp.bfloat16)
    result = middle + matmul(active, reduce_matrix) + reduce_offset.astype(jnp.float32)
    weight_mask = clip_mask.astype(jnp.float32)[:, None, None]
    layer_out = (result.reshape(count, local_length, width) * weight_mask).astype(jnp.bfloat16)
    (
        gain_first,
        shift_first,
        query_matrix,
        query_offset,
        key_matrix,
        value_matrix,
        value_offset,
        output_matrix,
        output_offset,
        gain_second,
        shift_second,
        expand_matrix,
        expand_offset,
        reduce_matrix,
        reduce_offset,
    ) = fetched
    grad_result = (cotangent.astype(jnp.float32) * weight_mask).reshape(tokens, width)
    grad_last = grad_result.astype(jnp.bfloat16)
    grad_reduce_offset = jnp.sum(grad_last.astype(jnp.float32), 0)
    grad_reduce_matrix = matmul_left_t(active, grad_last)
    grad_active = matmul_right_t(grad_last, reduce_matrix)
    grad_inner = gelu_pullback(grad_active)[0].astype(jnp.bfloat16)
    grad_expand_offset = jnp.sum(grad_inner.astype(jnp.float32), 0)
    grad_expand_matrix = matmul_left_t(hidden_two, grad_inner)
    grad_hidden_two = matmul_right_t(grad_inner, expand_matrix)
    grad_gain_second, grad_shift_second, grad_through = norm_back(
        grad_hidden_two, normed_two, inverse_two, gain_second.astype(jnp.float32)
    )
    grad_middle = grad_result + grad_through
    grad_branch = grad_middle.astype(jnp.bfloat16)
    grad_output_offset = jnp.sum(grad_branch.astype(jnp.float32), 0)
    grad_output_matrix = matmul_left_t(mixed, grad_branch)
    grad_mixed = matmul_right_t(grad_branch, output_matrix).astype(jnp.bfloat16)
    grad_mixed_heads = lax.all_to_all(
        grad_mixed.reshape(count, local_length, width),
        "seq",
        split_axis=2,
        concat_axis=1,
        tiled=True,
    )
    grad_query_heads, grad_key_heads, grad_value_heads = lax.map(
        attend_back, (query_heads, key_heads, value_heads, totals, grad_mixed_heads)
    )
    grad_query, grad_keys, grad_values = (
        lax.all_to_all(
            for_sending(grad_query_heads), "seq", split_axis=1, concat_axis=2, tiled=True
        ).astype(grad_query_heads.dtype),
        lax.all_to_all(grad_key_heads, "seq", split_axis=1, concat_axis=2, tiled=True),
        lax.all_to_all(grad_value_heads, "seq", split_axis=1, concat_axis=2, tiled=True),
    )
    grad_query = grad_query.reshape(tokens, width)
    grad_keys = grad_keys.reshape(tokens, width)
    grad_values = grad_values.reshape(tokens, width)
    grad_query_matrix = matmul_left_t(hidden_one, grad_query)
    grad_query_offset = jnp.sum(grad_query.astype(jnp.float32), 0)
    grad_key_matrix = matmul_left_t(hidden_one, grad_keys)
    grad_value_matrix = matmul_left_t(hidden_one, grad_values)
    grad_value_offset = jnp.sum(grad_values.astype(jnp.float32), 0)
    grad_hidden_one = (
        matmul_right_t(grad_query, query_matrix)
        + matmul_right_t(grad_keys, key_matrix)
        + matmul_right_t(grad_values, value_matrix)
    )
    grad_gain_first, grad_shift_first, grad_entry = norm_back(
        grad_hidden_one, normed_one, inverse_one, gain_first.astype(jnp.float32)
    )
    grad_clips = (grad_middle + grad_entry).astype(jnp.bfloat16).reshape(count, local_length, width)
    gradients = (
        grad_gain_first,
        grad_shift_first,
        grad_query_matrix,
        grad_query_offset,
        grad_key_matrix,
        grad_value_matrix,
        grad_value_offset,
        grad_output_matrix,
        grad_output_offset,
        grad_gain_second,
        grad_shift_second,
        grad_expand_matrix,
        grad_expand_offset,
        grad_reduce_matrix,
        grad_reduce_offset,
    )
    summed = (
        lax.psum_scatter(gradients[0], ("shard", "seq"), scatter_dimension=0, tiled=True),
        lax.psum_scatter(gradients[1], ("shard", "seq"), scatter_dimension=0, tiled=True),
        lax.psum_scatter(gradients[2], ("shard", "seq"), scatter_dimension=0, tiled=True),
        lax.psum_scatter(gradients[3], ("shard", "seq"), scatter_dimension=0, tiled=True),
        lax.psum_scatter(gradients[4], ("shard", "seq"), scatter_dimension=0, tiled=True),
        lax.psum_scatter(gradients[5], ("shard", "seq"), scatter_dimension=0, tiled=True),
        lax.psum_scatter(gradients[6], ("shard", "seq"), scatter_dimension=0, tiled=True),
        lax.psum_scatter(gradients[7], ("shard", "seq"), scatter_dimension=0, tiled=True),
        lax.psum_scatter(gradients[8], ("shard", "seq"), scatter_dimension=0, tiled=True),
        lax.psum_scatter(gradients[9], ("shard", "seq"), scatter_dimension=0, tiled=True),
        lax.psum_scatter(gradients[10], ("shard", "seq"), scatter_dimension=0, tiled=True),
        lax.psum_scatter(gradients[11], ("shard", "seq"), scatter_dimension=0, tiled=True),
        lax.psum_scatter(gradients[12], ("shard", "seq"), scatter_dimension=0, tiled=True),
        lax.psum_scatter(gradients[13], ("shard", "seq"), scatter_dimension=0, tiled=True),
        lax.psum_scatter(gradients[14], ("shard", "seq"), scatter_dimension=0, tiled=True),
    )
    return (
        layer_out,
        grad_clips,
        summed[0],
        summed[1],
        summed[2],
        summed[3],
        summed[4],
        summed[5],
        summed[6],
        summed[7],
        summed[8],
        summed[9],
        summed[10],
        summed[11],
        summed[12],
        summed[13],
        summed[14],
    )


def solution(mesh):
    return jax.shard_map(
        on_device,
        mesh=mesh,
        in_specs=(
            P("shard", "seq", None),
            P("shard"),
            P(("shard", "seq")),
            P(("shard", "seq")),
            P(("shard", "seq"), None),
            P(("shard", "seq")),
            P(("shard", "seq"), None),
            P(("shard", "seq"), None),
            P(("shard", "seq")),
            P(("shard", "seq"), None),
            P(("shard", "seq")),
            P(("shard", "seq")),
            P(("shard", "seq")),
            P(("shard", "seq"), None),
            P(("shard", "seq")),
            P(("shard", "seq"), None),
            P(("shard", "seq")),
            P("shard", "seq", None),
        ),
        out_specs=(
            P("shard", "seq", None),
            P("shard", "seq", None),
            P(("shard", "seq")),
            P(("shard", "seq")),
            P(("shard", "seq"), None),
            P(("shard", "seq")),
            P(("shard", "seq"), None),
            P(("shard", "seq"), None),
            P(("shard", "seq")),
            P(("shard", "seq"), None),
            P(("shard", "seq")),
            P(("shard", "seq")),
            P(("shard", "seq")),
            P(("shard", "seq"), None),
            P(("shard", "seq")),
            P(("shard", "seq"), None),
            P(("shard", "seq")),
        ),
        check_vma=False,
    )
```

profile of v0, /device:TPU:0, one launch (start us, length us, event | category | flops | bytes accessed | tf_op | source)
XLA Modules:
  0.0 1375.6 jit_solution(6295893765220282341)
XLA Ops:
  22.5 42.8 %all-reduce.18 = (bf16[1024]{0:T(1024)(128)(2,1)S(1)}, bf16[1024]{0:T(1024)(128)(2,1)S(1)}, bf16[1024]{0:T(1024)(128)(2,1)S(1)}, bf16[1024]{0:T(1024)(128)(2,1)S...) all-reduce(bf16[1024]{0:T(1024)(128)(2,1)S(1)} %dynamic-update-slic, ...), channel_id=1, replica_groups=mesh['shard'=8,'seq'=4] {'shard','seq'}, use_global_device_ids=true, to_apply=%add.2 | all-reduce | flops 8192 | bytes 32768
  67.0 3.6 all-gather.12.cloned.1.call-done
  70.6 3.7 fusion.49
  74.3 4.7 copy.75
  79.5 8.4 reduce.5
  87.9 4.2 reshape.305
  92.1 4.4 all-to-all-start.2
  96.5 33.0 %all-gather.10.cloned.1.call-done = bf16[1024,1024]{1,0:T(8,128)(2,1)} async-done(((bf16[32,1024]{1,0:T(8,128)(2,1)}), bf16[1024,1024]{1,0:T(8,128)(2,1)}) %all-gather.10.cloned.1.call-update) | async-done | bytes 2097168 | tf_op jit(solution)/shard_map/all_gather | solution.py:136
  129.5 3.7 fusion.48
  133.2 4.7 copy.72
  137.8 8.4 reduce.4
  146.3 4.2 reshape.303
  150.5 4.2 all-to-all-start.1
  155.9 32.4 %all-gather.8.cloned.1.call-done = bf16[1024,1024]{1,0:T(8,128)(2,1)} async-done(((bf16[32,1024]{1,0:T(8,128)(2,1)}), bf16[1024,1024]{1,0:T(8,128)(2,1)}) %all-gather.8.cloned.1.call-update) | async-done | bytes 2097168 | tf_op jit(solution)/shard_map/all_gather | solution.py:139
  188.3 3.7 fusion.47
  192.0 4.7 copy.69
  196.7 7.4 reduce.3
  206.9 3.8 reshape.306
  215.1 4.4 all-to-all-start
  219.5 3.9 reshape.304
  235.5 9.0 multiply_reduce_fusion.3
  244.5 4.5 copy-done
  249.0 4.1 fusion.1
  253.0 8.9 fusion
  261.9 3.9 reshape.302
  270.4 9.4 fusion.58
  279.9 9.3 fusion.57
  292.7 8.8 reduce.6
  306.8 48.2 %all-gather = bf16[32,1,128]{2,1,0:T(2,128)(2,1)S(1)} all-gather(bf16[1,1,128]{2,1,0:T(2,128)(2,1)S(1)} %convert_bitcast_fusion.1), channel_id=1, replica_groups=mesh['shard'=8,'seq'=4] {'shard','seq'}, dimensions={0}, use_global_device_ids=true | all-gather | bytes 8448 | tf_op jit(solution)/shard_map/all_gather | solution.py:146
  363.9 21.7 %multiply_convert_fusion.2 = (bf16[392,4096]{1,0:T(8,128)(2,1)}, f32[392,4096]{1,0:T(8,128)}, f32[392,4096]{1,0:T(8,128)}) fusion(f32[4096]{0:T(1024)S(1)} %bitcast.242, bf16[1024,4096]{1,0:T(8,128)(2,1)} %all-gather.16.cloned.1.call-done, f32[392,1024]{1,0:T(8,128)} %copy-done.11, f32[1024]{0:T(1024)S(1)} %convert_element_type.240, ...), kind=kOutput, calls=%fused_computation.24 | convolution fusion | flops 3396313088 | bytes 26078272 | tf_op jit(solution)/shard_map/dot_general | solution.py:17
  385.6 24.5 %all-gather.18.cloned.1.call-done = bf16[4096,1024]{1,0:T(8,128)(2,1)} async-done(((bf16[128,1024]{1,0:T(8,128)(2,1)}), bf16[4096,1024]{1,0:T(8,128)(2,1)}) %all-gather.18.cloned.1.call-update) | async-done | bytes 8388624 | tf_op jit(solution)/shard_map/all_gather | solution.py:147
  410.1 13.7 convert_reduce_fusion
  423.8 4.4 multiply_reduce_fusion.4
  435.5 4.2 copy.81
  439.7 8.3 reduce.7
  450.7 3.8 all-to-all-start.4
  454.6 16.1 %all-to-all-done.4 = bf16[4,2,50176]{2,1,0:T(2,128)(2,1)S(1)} async-done(((bf16[4,2,50176]{2,1,0:T(2,128)(2,1)}), bf16[4,2,50176]{2,1,0:T(2,128)(2,1)S(1)}, u32[]{:S(2)}, u32[]{:S(2)}) %all-to-all-start.4) | async-done | bytes 802848 | tf_op jit(solution)/shard_map/all_to_all | solution.py:291
  470.7 3.6 reshape.310
  474.3 4.6 copy.82
  483.2 9.1 fusion.4
  492.3 9.9 fusion.20
  502.3 4.8 copy.89
  507.1 9.6 reduce.8
  522.3 24.6 %multiply_reduce_fusion.1 = (f32[4,784]{1,0:T(4,128)S(1)}, f32[4,784,1568]{2,1,0:T(8,128)}) fusion(f32[4,784,1568]{2,1,0:T(8,128)} %get-tuple-element.99, f32[4,784]{1,0:T(4,128)S(1)} %log_add_fusion.1, bf16[784,4,64]{0,2,1:T(8,128)(2,1)S(1)} %slice.41, bf16[1568,4,64]{0,2,1:T(8,128)(2,1)S(1)} %reshape.271), kind=kOutput, calls=%fused_computation.4 | convolution fusion | flops 649073600 | bytes 40567296 | tf_op jit(solution)/shard_map/while/body/eval_jaxpr/qhd,khd->hqk/dot_general | solution.py:100
  555.6 14.5 %multiply_convert_fusion.1 = bf16[4,784,1568]{2,1,0:T(8,128)(2,1)S(1)} fusion(f32[4,784,1568]{2,1,0:T(8,128)} %get-tuple-element.107, f32[4,784,1568]{2,1,0:T(8,128)} %get-tuple-element.99, f32[4,784]{1,0:T(4,128)S(1)} %get-tuple-element.106, f32[4,784]{1,0:T(4,128)S(1)} %log_add_fusion.1), kind=kLoop, calls=%fused_computation.3 | loop fusion | flops 24586240 | bytes 49197568 | tf_op jit(solution)/shard_map/while/body/eval_jaxpr/convert_element_type | solution.py:104
  570.1 3.9 copy-done.1
  575.7 13.5 multiply_reduce_fusion
  589.2 14.4 %multiply_convert_fusion = bf16[4,784,1568]{2,1,0:T(8,128)(2,1)S(1)} fusion(f32[4,784,1568]{2,1,0:T(8,128)} %get-tuple-element.105, f32[4,784,1568]{2,1,0:T(8,128)} %copy-done, f32[4,784]{1,0:T(4,128)S(1)} %get-tuple-element.104, f32[4,784]{1,0:T(4,128)S(1)} %log_add_fusion), kind=kLoop, calls=%fused_computation | loop fusion | flops 24586240 | bytes 49197568 | tf_op jit(solution)/shard_map/while/body/eval_jaxpr/convert_element_type | solution.py:104
  607.8 4.8 copy.87
  612.6 9.6 reduce.10
  623.5 18.7 %all_to_all.120 = bf16[4,2,50176]{2,1,0:T(2,128)(2,1)} all-to-all(bf16[4,2,50176]{2,1,0:T(2,128)(2,1)S(1)} %reshape.313), channel_id=1, replica_groups=mesh['shard'=8,'seq'=4] {'seq'}, dimensions={0} | all-to-all | bytes 1605632 | tf_op jit(solution)/shard_map/all_to_all | solution.py:305
  645.2 3.6 fusion.74
  650.0 7.2 fusion.56
  657.1 7.2 fusion.55
  667.9 8.8 reduce.9
  676.9 17.3 %all_to_all.121 = bf16[4,2,50176]{2,1,0:T(2,128)(2,1)S(1)} all-to-all(bf16[4,2,50176]{2,1,0:T(2,128)(2,1)S(1)} %reshape.311), channel_id=1, replica_groups=mesh['shard'=8,'seq'=4] {'seq'}, dimensions={0} | all-to-all | bytes 1605632 | tf_op jit(solution)/shard_map/all_to_all | solution.py:302
  703.4 12.9 fusion.70
  717.5 10.1 fusion.61
  728.3 9.3 fusion.46
  744.5 43.1 %all-reduce.17 = (f32[1024]{0:T(1024)S(1)}, f32[1024]{0:T(1024)S(1)}, f32[1024]{0:T(1024)S(1)}, f32[1024]{0:T(1024)S(1)}, f32[1024]{0:T(1024)S(1)}, /*index=5*/f...) all-reduce(f32[1024]{0:T(1024)S(1)} %get-tuple-element.64, ...), channel_id=2, replica_groups=mesh['shard'=8,'seq'=4] {'shard','seq'}, use_global_device_ids=true, to_apply=%region_15.16.clone | all-reduce | flops 12288 | bytes 98304
  795.8 62.5 %reduce-scatter.9.cloned.1.call-done = f32[32,1024]{1,0:T(8,128)} async-done(((f32[1024,1024]{1,0:T(8,128)}), f32[32,1024]{1,0:T(8,128)}) %reduce-scatter.9.cloned.1.call-update) | async-done | bytes 131088 | tf_op jit(solution)/shard_map/reduce_scatter | solution.py:347
  858.3 140.8 %reduce-scatter.7.cloned.1.call-done = f32[32,1024]{1,0:T(8,128)} async-done(((f32[1024,1024]{1,0:T(8,128)}), f32[32,1024]{1,0:T(8,128)}) %reduce-scatter.7.cloned.1.call-update) | async-done | bytes 131088 | tf_op jit(solution)/shard_map/reduce_scatter | solution.py:345
  999.2 182.0 %reduce-scatter.15.cloned.1.call-done = f32[32,4096]{1,0:T(8,128)} async-done(((f32[1024,4096]{1,0:T(8,128)}), f32[32,4096]{1,0:T(8,128)}) %reduce-scatter.15.cloned.1.call-update) | async-done | bytes 524304 | tf_op jit(solution)/shard_map/reduce_scatter | solution.py:354
  1181.2 187.4 %reduce-scatter.17.cloned.1.call-done = f32[128,1024]{1,0:T(8,128)} async-done(((f32[4096,1024]{1,0:T(8,128)}), f32[128,1024]{1,0:T(8,128)}) %reduce-scatter.17.cloned.1.call-update) | async-done | bytes 524304 | tf_op jit(solution)/shard_map/reduce_scatter | solution.py:356
  (261 shorter events, 129.0 us)
Async XLA Ops:
  7.2 59.5 %copy-start.7 = (bf16[1,392,1024]{2,1,0:T(8,128)(2,1)S(1)}, bf16[1,392,1024]{2,1,0:T(8,128)(2,1)}, u32[]{:S(2)}) copy-start(bf16[1,392,1024]{2,1,0:T(8,128)(2,1)} %param.18) | copy-start | bytes 2408452
  7.2 63.4 %all-gather.12.cloned.1.call-start = ((), (), s32[]{:S(2)}) async-start(), calls=%async_computation.16 | async-start | bytes 2162688 | tf_op jit(solution)/shard_map/all_gather | solution.py:138
  8.9 120.6 %all-gather.10.cloned.1.call-start = ((), (), s32[]{:S(2)}) async-start(), calls=%async_computation.15 | async-start | bytes 2162688 | tf_op jit(solution)/shard_map/all_gather | solution.py:136
  10.5 177.8 %all-gather.8.cloned.1.call-start = ((), (), s32[]{:S(2)}) async-start(), calls=%async_computation.14 | async-start | bytes 2162688 | tf_op jit(solution)/shard_map/all_gather | solution.py:139
  12.1 347.5 %all-gather.14.cloned.1.call-start = ((), (), s32[]{:S(2)}) async-start(), calls=%async_computation.17 | async-start | bytes 2162688 | tf_op jit(solution)/shard_map/all_gather | solution.py:141
  13.7 350.2 %all-gather.16.cloned.1.call-start = ((), (), s32[]{:S(2)}) async-start(), calls=%async_computation.18 | async-start | bytes 8650752 | tf_op jit(solution)/shard_map/all_gather | solution.py:145
  65.3 123.0 %copy-start.34 = (f32[1024]{0:T(1024)}, f32[1024]{0:T(1024)S(1)}, u32[]{:S(2)}) copy-start(f32[1024]{0:T(1024)S(1)} %convert_element_type.214) | copy-start | bytes 12292
  65.3 123.0 %copy-start.40 = (f32[1024]{0:T(1024)}, f32[1024]{0:T(1024)S(1)}, u32[]{:S(2)}) copy-start(f32[1024]{0:T(1024)S(1)} %convert_element_type.216) | copy-start | bytes 12292
  66.6 121.7 %copy-start.29 = (f32[392]{0:T(512)}, f32[392]{0:T(512)S(1)}, u32[]{:S(2)}) copy-start(f32[392]{0:T(512)S(1)} %broadcast_multiply_fusion.5) | copy-start | bytes 4708
  67.0 121.3 %copy-start.36 = (f32[392]{0:T(512)}, f32[392]{0:T(512)S(1)}, u32[]{:S(2)}) copy-start(f32[392]{0:T(512)S(1)} %add_rsqrt_fusion.1) | copy-start | bytes 4708
  92.1 58.4 %all-to-all-start.2 = ((bf16[4,2,50176]{2,1,0:T(2,128)(2,1)}), bf16[4,2,50176]{2,1,0:T(2,128)(2,1)}, u32[]{:S(2)}, u32[]{:S(2)}) async-start(bf16[4,2,50176]{2,1,0:T(2,128)(2,1)} %reshape.305), calls=%async_computation.2 | async-start | bytes 1605632 | tf_op jit(solution)/shard_map/all_to_all | solution.py:229
  137.8 17.3 %copy-start.28 = (f32[128,1024]{1,0:T(8,128)S(1)}, f32[128,1024]{1,0:T(8,128)}, u32[]{:S(2)}) copy-start(f32[128,1024]{1,0:T(8,128)} %param.33) | copy-start | bytes 1572868
  150.5 64.6 %all-to-all-start.1 = ((bf16[4,2,50176]{2,1,0:T(2,128)(2,1)}), bf16[4,2,50176]{2,1,0:T(2,128)(2,1)}, u32[]{:S(2)}, u32[]{:S(2)}) async-start(bf16[4,2,50176]{2,1,0:T(2,128)(2,1)} %reshape.303), calls=%async_computation.1 | async-start | bytes 1605632 | tf_op jit(solution)/shard_map/all_to_all | solution.py:222
  154.7 255.4 %all-gather.18.cloned.1.call-start = ((), (), s32[]{:S(2)}) async-start(), calls=%async_computation.19 | async-start | bytes 8650752 | tf_op jit(solution)/shard_map/all_gather | solution.py:147
  215.1 20.4 %copy-start.3 = (bf16[1568,4,64]{0,2,1:T(8,128)(2,1)}, bf16[1568,4,64]{0,2,1:T(8,128)(2,1)S(1)}, u32[]{:S(2)}) copy-start(bf16[1568,4,64]{0,2,1:T(8,128)(2,1)S(1)} %reshape.274) | copy-start | bytes 2408452
  215.1 46.8 %all-to-all-start = ((bf16[4,2,50176]{2,1,0:T(2,128)(2,1)}), bf16[4,2,50176]{2,1,0:T(2,128)(2,1)}, u32[]{:S(2)}, u32[]{:S(2)}) async-start(bf16[4,2,50176]{2,1,0:T(2,128)(2,1)} %reshape.301), calls=%async_computation | async-start | bytes 1605632 | tf_op jit(solution)/shard_map/all_to_all | solution.py:232
  230.9 4.7 copy-start.17
  232.5 3.1 copy-start.15
  235.5 13.4 copy-start
  292.7 14.0 %copy-start.49 = (f32[128]{0:T(128)S(1)}, f32[128]{0:T(128)}, u32[]{:S(2)}) copy-start(f32[128]{0:T(128)} %param.32) | copy-start | bytes 1540
  302.5 52.5 %all-to-all-start.3 = ((bf16[4,2,50176]{2,1,0:T(2,128)(2,1)}), bf16[4,2,50176]{2,1,0:T(2,128)(2,1)S(1)}, u32[]{:S(2)}, u32[]{:S(2)}) async-start(bf16[4,2,50176]{2,1,0:T(2,128)(2,1)} %reshape.307), calls=%async_computation.3 | async-start | bytes 1605632 | tf_op jit(solution)/shard_map/all_to_all | solution.py:242
  306.0 489.8 %reduce-scatter.13.cloned.1.call-start = ((), (), s32[]{:S(2)}) async-start(), calls=%async_computation.23 | async-start | bytes 4325376 | tf_op jit(solution)/shard_map/reduce_scatter | solution.py:350
  306.7 57.2 %copy-start.42 = (f32[1024]{0:T(1024)}, f32[1024]{0:T(1024)S(1)}, u32[]{:S(2)}) copy-start(f32[1024]{0:T(1024)S(1)} %convert_element_type.240) | copy-start | bytes 12292
  357.4 2.1 copy-start.8
  362.3 1.2 copy-start.11
  363.9 46.2 %copy-start.19 = (bf16[1,392,1024]{2,1,0:T(8,128)(2,1)S(1)}, bf16[1,392,1024]{2,1,0:T(8,128)(2,1)}, u32[]{:S(2)}) copy-start(bf16[1,392,1024]{2,1,0:T(8,128)(2,1)} %param.35) | copy-start | bytes 2408452
  410.1 13.7 copy-start.12
  410.1 13.7 copy-start.45
  423.8 4.4 copy-start.50
  423.8 4.4 copy-start.20
  429.6 3.3 copy-start.5
  450.7 20.0 %all-to-all-start.4 = ((bf16[4,2,50176]{2,1,0:T(2,128)(2,1)}), bf16[4,2,50176]{2,1,0:T(2,128)(2,1)S(1)}, u32[]{:S(2)}, u32[]{:S(2)}) async-start(bf16[4,2,50176]{2,1,0:T(2,128)(2,1)} %reshape.309), calls=%async_computation.4 | async-start | bytes 1605632 | tf_op jit(solution)/shard_map/all_to_all | solution.py:291
  483.2 9.1 copy-start.13
  518.7 28.2 %all-to-all-start.7 = ((bf16[4,2,50176]{2,1,0:T(2,128)(2,1)}), bf16[4,2,50176]{2,1,0:T(2,128)(2,1)S(1)}, u32[]{:S(2)}, u32[]{:S(2)}) async-start(bf16[4,2,50176]{2,1,0:T(2,128)(2,1)} %reshape.315), calls=%async_computation.7 | async-start | bytes 1605632 | tf_op jit(solution)/shard_map/all_to_all | solution.py:306
  522.2 273.6 %reduce-scatter.11.cloned.1.call-start = ((), (), s32[]{:S(2)}) async-start(), calls=%async_computation.22 | async-start | bytes 4325376 | tf_op jit(solution)/shard_map/reduce_scatter | solution.py:348
  548.9 3.0 copy-start.9
  548.9 3.0 copy-start.30
  548.9 3.0 copy-start.35
  548.9 3.0 copy-start.37
  548.9 3.0 copy-start.41
  555.5 302.8 %reduce-scatter.9.cloned.1.call-start = ((), (), s32[]{:S(2)}) async-start(), calls=%async_computation.21 | async-start | bytes 4325376 | tf_op jit(solution)/shard_map/reduce_scatter | solution.py:347
  555.6 18.4 %copy-start.18 = (bf16[784,4,64]{0,2,1:T(8,128)(2,1)S(1)}, bf16[784,4,64]{0,2,1:T(8,128)(2,1)}, u32[]{:S(2)}) copy-start(bf16[784,4,64]{0,2,1:T(8,128)(2,1)} %copy-done.17) | copy-start | bytes 1204228
  570.1 3.9 copy-start.1
  574.0 1.8 copy-start.14
  589.2 14.4 %copy-start.16 = (bf16[784,4,64]{0,2,1:T(8,128)(2,1)S(1)}, bf16[784,4,64]{0,2,1:T(8,128)(2,1)}, u32[]{:S(2)}) copy-start(bf16[784,4,64]{0,2,1:T(8,128)(2,1)} %copy-done.15) | copy-start | bytes 1204228
  603.6 4.2 copy-start.2
  645.2 3.6 copy-start.24
  648.8 1.2 copy-start.4
  648.8 350.4 %reduce-scatter.7.cloned.1.call-start = ((), (), s32[]{:S(2)}) async-start(), calls=%async_computation.20 | async-start | bytes 4325376 | tf_op jit(solution)/shard_map/reduce_scatter | solution.py:345
  696.2 3.0 copy-start.10
  702.8 478.4 %reduce-scatter.15.cloned.1.call-start = ((), (), s32[]{:S(2)}) async-start(), calls=%async_computation.24 | async-start | bytes 17301504 | tf_op jit(solution)/shard_map/reduce_scatter | solution.py:354
  716.3 1.1 copy-start.21
  716.4 652.2 %reduce-scatter.17.cloned.1.call-start = ((), (), s32[]{:S(2)}) async-start(), calls=%async_computation.25 | async-start | bytes 17301504 | tf_op jit(solution)/shard_map/reduce_scatter | solution.py:356
  728.3 9.6 copy-start.27
  728.3 9.6 copy-start.47
  737.9 1.1 copy-start.25
  737.9 1.9 copy-start.46
  739.8 1.9 copy-start.48
  741.6 2.8 copy-start.31
  741.6 2.8 copy-start.32
  741.6 2.8 copy-start.33
  741.6 2.8 copy-start.38
  741.7 2.8 copy-start.39
  741.7 51.2 %copy-start.6 = (f32[392,1024]{1,0:T(8,128)S(1)}, f32[392,1024]{1,0:T(8,128)}, u32[]{:S(2)}) copy-start(f32[392,1024]{1,0:T(8,128)} %copy-done.5) | copy-start | bytes 4816900
  (5 other events, 4.3 us)
Sparse Core Ops, SparseCore 0:
  11.4 59.1 all-gather.11
  74.1 55.3 all-gather.9
  132.9 55.3 all-gather.7
  191.6 55.0 all-gather.13
  250.0 81.6 all-gather.15
  334.4 75.6 all-gather.17
  433.0 142.0 reduce-scatter.12
  577.9 138.9 reduce-scatter.10
  719.8 138.5 reduce-scatter.8
  861.0 138.1 reduce-scatter.6
  1002.1 179.0 reduce-scatter.14
  1183.9 184.5 reduce-scatter.16
where the time goes:
time: 1380 us
  waiting for transfers between devices  683 us (49%)
  matrix products  215 us (16%)
  blocking collectives  170 us (12%)
  local copies, waits for them, and re-layouts  135 us (10%)
  other arithmetic  132 us (10%)
  starting transfers between devices  24.9 us (2%)
  between operations  16.1 us (1%)
    reduce_scatter x1, waiting for transfers between devices, on_device(): lax.psum_scatter(gradients[13], ('shard', 'seq'), scatter_dimension=0, ti...  187 us
    reduce_scatter x1, waiting for transfers between devices, on_device(): lax.psum_scatter(gradients[11], ('shard', 'seq'), scatter_dimension=0, ti...  182 us
    reduce_scatter x1, waiting for transfers between devices, on_device(): lax.psum_scatter(gradients[2], ('shard', 'seq'), scatter_dimension=0, til...  141 us
    unnamed x2, blocking collectives  86 us
    unnamed x154, local copies, waits for them, and re-layouts  72.7 us
    unnamed x9, other arithmetic  69.2 us
    reduce_scatter x1, waiting for transfers between devices, on_device(): lax.psum_scatter(gradients[4], ('shard', 'seq'), scatter_dimension=0, til...  62.5 us
    all_gather x1, blocking collectives, fetch_first(): lax.all_gather(masters[12].astype(jnp.bfloat16), ('shard', 'seq'), axis=0...  48.2 us
  transfers between devices with their start and end apart: 18, of which 9 were waited for; matrix products, arithmetic and copies ran while one was open for 32% of the time, Pallas kernels for 0%

commit v1 on v0

v1 whole, which is shorter than its diff:
```python
import jax
import jax.numpy as jnp
from jax import lax
from jax.sharding import PartitionSpec as P

HEAD_DIM = 64


EPSILON = 1e-06


def for_sending(value):
    return jax.tree.map(lambda a: a.astype(jnp.bfloat16) if a.dtype == jnp.float32 else a, value)


def matmul(left, right):
    return jnp.dot(left, right, preferred_element_type=jnp.float32)


def matmul_right_t(left, right):
    return lax.dot_general(
        left, right, (((1,), (1,)), ((), ())), preferred_element_type=jnp.float32
    )


def matmul_left_t(left, right):
    return lax.dot_general(
        left, right, (((0,), (0,)), ((), ())), preferred_element_type=jnp.float32
    )


def gelu_exact(values):
    return jax.nn.gelu(values, approximate=False)


def normalize(values):
    average = jnp.mean(values, -1, keepdims=True)
    centred = values - average
    variance = jnp.mean(centred * centred, -1, keepdims=True)
    inverse = lax.rsqrt(variance + EPSILON)
    return (centred * inverse, inverse)


def norm_back(grad_normed, normed, inverse, gain):
    grad_gain = jnp.sum(grad_normed * normed, 0)
    grad_shift = jnp.sum(grad_normed, 0)
    scaled = grad_normed * gain
    plain_mean = jnp.mean(scaled, -1, keepdims=True)
    cross_mean = jnp.mean(scaled * normed, -1, keepdims=True)
    return (grad_gain, grad_shift, inverse * (scaled - plain_mean - normed * cross_mean))


def attend_clip(inputs):
    query, keys, values = inputs
    length = query.shape[0]
    heads = query.shape[1] // HEAD_DIM
    scale = HEAD_DIM ** (-0.5)
    query = query.reshape(length, heads, HEAD_DIM)
    keys = keys.reshape(length, heads, HEAD_DIM)
    values = values.reshape(length, heads, HEAD_DIM)
    half = length // 2
    outputs = []
    totals = []
    for block in range(2):
        rows_query = query[block * half : (block + 1) * half]
        scores = (
            jnp.einsum("qhd,khd->hqk", rows_query, keys, preferred_element_type=jnp.float32) * scale
        )
        row_max = jnp.max(scores, -1, keepdims=True)
        raised = jnp.exp(scores - row_max)
        summed = jnp.sum(raised, -1, keepdims=True)
        probs = (raised / summed).astype(jnp.bfloat16)
        mixed = jnp.einsum("hqk,khd->qhd", probs, values, preferred_element_type=jnp.float32)
        outputs.append(mixed.astype(jnp.bfloat16))
        totals.append((row_max + jnp.log(summed))[..., 0])
    joined = jnp.concatenate(outputs, 0).reshape(length, heads * HEAD_DIM)
    return (joined, jnp.concatenate(totals, 1))


def attend_back(inputs):
    query, keys, values, totals, grad_out = inputs
    length = query.shape[0]
    heads = query.shape[1] // HEAD_DIM
    scale = HEAD_DIM ** (-0.5)
    query = query.reshape(length, heads, HEAD_DIM)
    keys = keys.reshape(length, heads, HEAD_DIM)
    values = values.reshape(length, heads, HEAD_DIM)
    grad_out = grad_out.reshape(length, heads, HEAD_DIM)
    half = length // 2
    grad_keys = jnp.zeros((length, heads, HEAD_DIM), jnp.float32)
    grad_values = jnp.zeros((length, heads, HEAD_DIM), jnp.float32)
    query_parts = []
    for block in range(2):
        rows_query = query[block * half : (block + 1) * half]
        rows_grad = grad_out[block * half : (block + 1) * half]
        scores = (
            jnp.einsum("qhd,khd->hqk", rows_query, keys, preferred_element_type=jnp.float32) * scale
        )
        probs = jnp.exp(scores - totals[:, block * half : (block + 1) * half, None])
        grad_probs = jnp.einsum(
            "qhd,khd->hqk", rows_grad, values, preferred_element_type=jnp.float32
        )
        weighted = jnp.sum(probs * grad_probs, -1, keepdims=True)
        grad_scores = (probs * (grad_probs - weighted)).astype(jnp.bfloat16)
        part = (
            jnp.einsum("hqk,khd->qhd", grad_scores, keys, preferred_element_type=jnp.float32)
            * scale
        )
        query_parts.append(part.astype(jnp.bfloat16))
        grad_keys = (
            grad_keys
            + jnp.einsum(
                "hqk,qhd->khd", grad_scores, rows_query, preferred_element_type=jnp.float32
            )
            * scale
        )
        grad_values = grad_values + jnp.einsum(
            "hqk,qhd->khd",
            probs.astype(jnp.bfloat16),
            rows_grad,
            preferred_element_type=jnp.float32,
        )
    width = heads * HEAD_DIM
    grad_query = jnp.concatenate(query_parts, 0).reshape(length, width)
    return (
        grad_query,
        grad_keys.astype(jnp.bfloat16).reshape(length, width),
        grad_values.astype(jnp.bfloat16).reshape(length, width),
    )


def tensor_parallel(shards, seqs):
    axes = ("shard", "seq")

    def run(
        clips, clip_mask, norm1_gain, norm1_shift, query_weight, query_bias, key_weight,
        value_weight, value_bias, out_weight, out_bias, norm2_gain, norm2_shift, fc1_weight,
        fc1_bias, fc2_weight, fc2_bias, cotangent,
    ):
        low = jnp.bfloat16
        wide = jnp.float32
        _, local, width = clips.shape
        rows = query_weight.shape[0]
        hidden_rows, hidden_local = fc2_weight.shape[0], fc1_weight.shape[1] // seqs
        part = width // seqs
        heads = part // HEAD_DIM
        length = local * seqs
        place = lax.axis_index("seq")
        projections = jnp.stack([query_weight, key_weight, value_weight], 1).astype(low)
        projections = projections.reshape(rows, 3, seqs, part).transpose(2, 0, 1, 3)
        expand = fc1_weight.astype(low).reshape(rows, shards, seqs, hidden_rows)
        expand = expand.transpose(2, 0, 1, 3)
        outward = jnp.concatenate(
            [projections.reshape(seqs, rows, 3 * part), expand.reshape(seqs, rows, hidden_local)], -1
        )
        inward = lax.all_to_all(outward, "seq", 0, 0, tiled=True).reshape(seqs * rows, -1)
        packed = lax.all_gather(inward, "shard", axis=0, tiled=True)
        projection, expand_matrix = packed[:, : 3 * part], packed[:, 3 * part :]
        reduce_matrix = lax.all_gather(fc2_weight.astype(low), "shard", axis=0, tiled=True)
        output_matrix = lax.all_gather(out_weight.astype(low), axes, axis=0, tiled=True)
        small = jnp.stack(
            [norm1_gain, norm1_shift, query_bias, value_bias, out_bias, norm2_gain, norm2_shift, fc2_bias]
        ).astype(low)
        small = lax.all_gather(small, axes, axis=1, tiled=True).astype(wide)
        gain_one, shift_one, bias_q, bias_v, bias_o, gain_two, shift_two, bias_r = small
        bias_e = lax.all_gather(fc1_bias.astype(low), "shard", axis=0, tiled=True).astype(wide)

        inputs = clips[0].astype(wide)
        normed_one, inverse_one = normalize(inputs)
        hidden_one = (normed_one * gain_one + shift_one).astype(low)
        hidden_one = lax.all_gather(hidden_one, "seq", axis=0, tiled=True)
        own = lambda vector: lax.dynamic_slice(vector, (place * part,), (part,))
        bias = jnp.concatenate([own(bias_q), jnp.zeros((part,), wide), own(bias_v)])
        qkv = (matmul(hidden_one, projection) + bias).astype(low)
        query, keys, values = qkv[:, :part], qkv[:, part : 2 * part], qkv[:, 2 * part :]
        mixed_heads, totals = attend_clip((query, keys, values))
        mixed = lax.all_to_all(mixed_heads, "seq", 0, 1, tiled=True)
        middle = inputs + matmul(mixed, output_matrix) + bias_o
        normed_two, inverse_two = normalize(middle)
        hidden_two = (normed_two * gain_two + shift_two).astype(low)
        hidden_two = lax.all_gather(hidden_two, "seq", axis=0, tiled=True)

        mask = clip_mask[0].astype(wide)
        grad_result = cotangent[0].astype(wide) * mask
        grad_last = grad_result.astype(low)
        grad_reduce_bias = jnp.sum(grad_last.astype(wide), 0)
        grad_last = lax.all_gather(grad_last, "seq", axis=0, tiled=True)
        inner = matmul(hidden_two, expand_matrix) + bias_e
        active_float, pullback = jax.vjp(gelu_exact, inner)
        active = active_float.astype(low)
        result = lax.psum_scatter(
            matmul(active, reduce_matrix).astype(low), "seq", scatter_dimension=0, tiled=True
        )
        layer_out = ((middle + result.astype(wide) + bias_r) * mask).astype(low)[None]
        grad_reduce = matmul_left_t(active, grad_last)
        grad_inner = pullback(matmul_right_t(grad_last, reduce_matrix))[0].astype(low)
        grad_expand_bias = jnp.sum(grad_inner.astype(wide), 0)
        grad_expand = matmul_left_t(hidden_two, grad_inner)
        grad_hidden_two = lax.psum_scatter(
            matmul_right_t(grad_inner, expand_matrix).astype(low), "seq", scatter_dimension=0, tiled=True
        ).astype(wide)
        grad_gain_two, grad_shift_two, grad_through = norm_back(
            grad_hidden_two, normed_two, inverse_two, gain_two
        )
        grad_middle = grad_result + grad_through
        grad_branch = grad_middle.astype(low)
        grad_output_bias = jnp.sum(grad_branch.astype(wide), 0)
        grad_output = matmul_left_t(mixed, grad_branch)
        grad_mixed = matmul_right_t(grad_branch, output_matrix).astype(low)
        grad_mixed = lax.all_to_all(grad_mixed, "seq", 1, 0, tiled=True)

        grads = attend_back((query, keys, values, totals, grad_mixed))
        grad_qkv = jnp.concatenate(grads, 1)
        grad_projection = matmul_left_t(hidden_one, grad_qkv)
        grad_bias = jnp.sum(grad_qkv.astype(wide), 0)
        grad_hidden_one = lax.psum_scatter(
            matmul_right_t(grad_qkv, projection).astype(low), "seq", scatter_dimension=0, tiled=True
        ).astype(wide)
        grad_gain_one, grad_shift_one, grad_entry = norm_back(
            grad_hidden_one, normed_one, inverse_one, gain_one
        )
        grad_clips = (grad_middle + grad_entry).astype(low)[None]

        spread = lambda v: lax.dynamic_update_slice(jnp.zeros((width,), wide), v, (place * part,))
        small = jnp.stack(
            [
                grad_gain_one, grad_shift_one, spread(grad_bias[:part]), spread(grad_bias[2 * part :]),
                grad_output_bias, grad_gain_two, grad_shift_two, grad_reduce_bias,
            ]
        )
        small = lax.psum_scatter(small, axes, scatter_dimension=1, tiled=True)
        grad_expand_bias = lax.psum_scatter(grad_expand_bias, "shard", scatter_dimension=0, tiled=True)
        packed = jnp.concatenate([grad_projection, grad_expand], 1).astype(low)
        packed = lax.psum_scatter(packed, "shard", scatter_dimension=0, tiled=True)
        packed = lax.all_to_all(packed.reshape(seqs, rows, -1), "seq", 0, 0, tiled=True).astype(wide)
        grad_qkv_rows = packed[..., : 3 * part].reshape(seqs, rows, 3, part).transpose(2, 1, 0, 3)
        grad_qkv_rows = grad_qkv_rows.reshape(3, rows, width)
        grad_expand = packed[..., 3 * part :].reshape(seqs, rows, shards, hidden_rows)
        grad_expand = grad_expand.transpose(1, 2, 0, 3).reshape(rows, -1)
        grad_reduce = lax.psum_scatter(
            grad_reduce.astype(low), "shard", scatter_dimension=0, tiled=True
        ).astype(wide)
        grad_output = lax.psum_scatter(
            grad_output.astype(low), axes, scatter_dimension=0, tiled=True
        ).astype(wide)
        return (
            layer_out, grad_clips, small[0], small[1], grad_qkv_rows[0], small[2], grad_qkv_rows[1],
            grad_qkv_rows[2], small[3], grad_output, small[4], small[5], small[6], grad_expand,
            grad_expand_bias, grad_reduce, small[7],
        )

    return run


def solution(mesh):
    return jax.shard_map(
        tensor_parallel(mesh.shape["shard"], mesh.shape["seq"]),
        mesh=mesh,
        in_specs=(
            P("shard", "seq", None),
            P("shard"),
            P(("shard", "seq")),
            P(("shard", "seq")),
            P(("shard", "seq"), None),
            P(("shard", "seq")),
            P(("shard", "seq"), None),
            P(("shard", "seq"), None),
            P(("shard", "seq")),
            P(("shard", "seq"), None),
            P(("shard", "seq")),
            P(("shard", "seq")),
            P(("shard", "seq")),
            P(("shard", "seq"), None),
            P(("shard", "seq")),
            P(("shard", "seq"), None),
            P(("shard", "seq")),
            P("shard", "seq", None),
        ),
        out_specs=(
            P("shard", "seq", None),
            P("shard", "seq", None),
            P(("shard", "seq")),
            P(("shard", "seq")),
            P(("shard", "seq"), None),
            P(("shard", "seq")),
            P(("shard", "seq"), None),
            P(("shard", "seq"), None),
            P(("shard", "seq")),
            P(("shard", "seq"), None),
            P(("shard", "seq")),
            P(("shard", "seq")),
            P(("shard", "seq")),
            P(("shard", "seq"), None),
            P(("shard", "seq")),
            P(("shard", "seq"), None),
            P(("shard", "seq")),
        ),
        check_vma=False,
    )
```

time: 1380 us -> 947 us (0.69)
  waiting for transfers between devices: 683 us -> 498 us
  local copies, waits for them, and re-layouts: 135 us -> 39.5 us
  blocking collectives: 170 us -> 113 us
  matrix products: 215 us -> 172 us
  other arithmetic: 132 us -> 93 us
  starting transfers between devices: 24.9 us -> 8.76 us
    reduce_scatter x6, waiting for transfers between devices: 573 us -> 205 us  [the longest x1 81.3 us: run(): packed = lax.psum_scatter(packed, 'shard', scatter_dimension=0, tiled=True)]
    unnamed x12 -> x14, waiting for transfers between devices: 0.2 us -> 132 us
    unnamed x9 -> x2, other arithmetic: 69.2 us -> 0.01 us
    unnamed x2 -> x1, blocking collectives: 86 us -> 21.2 us
    all_gather x6, waiting for transfers between devices: 93.5 us -> 152 us  [the longest x1 64.7 us: run(): packed = lax.all_gather(inward, 'shard', axis=0, tiled=True)]
    unnamed x154 -> x112, local copies, waits for them, and re-layouts: 72.7 us -> 24 us
    dot_general x6 -> x4, matrix products: 44.8 us -> 21.7 us  [matmul(): return jnp.dot(left, right, preferred_element_type=jnp.float32)]
    reshape x6, local copies, waits for them, and re-layouts: 20 us -> 1.76 us  [the longest x1 1.01 us: run(): grad_expand = grad_expand.transpose(1, 2, 0, 3).reshape(rows, -1)]
  transfers between devices with their start and end apart: 18 -> 15, of which waited for: 9 -> 12; matrix products, arithmetic and copies ran while one was open for 32% -> 26% of each run, Pallas kernels for 0% -> 0%
where the time goes in v1:
time: 947 us; the launch traced here: 941 us
  waiting for transfers between devices  498 us (53%)
  matrix products  172 us (18%)
  blocking collectives  113 us (12%)
  other arithmetic  93 us (10%)
  local copies, waits for them, and re-layouts  39.5 us (4%)
  between operations  16.5 us (2%)
    unnamed x14, waiting for transfers between devices  132 us
    reduce_scatter x1, waiting for transfers between devices, run(): packed = lax.psum_scatter(packed, 'shard', scatter_dimension=0, tiled=True)  81.3 us
    all_gather x1, waiting for transfers between devices, run(): packed = lax.all_gather(inward, 'shard', axis=0, tiled=True)  64.7 us
    all_gather x1, blocking collectives, run(): small = lax.all_gather(small, axes, axis=1, tiled=True).astype(wide)  43.4 us
    all_gather x1, waiting for transfers between devices, run(): lax.all_gather(fc2_weight.astype(low), 'shard', axis=0, tiled=True)  42.8 us
    reduce_scatter x1, waiting for transfers between devices, run(): lax.psum_scatter(matmul(active, reduce_matrix).astype(low), 'seq', scatte...  38.9 us
    dot_general x4, matrix products, matmul_right_t(): lax.dot_general(left, right, (((1,), (1,)), ((), ())), preferred_element_...  35.4 us
    reduce_scatter x1, waiting for transfers between devices, run(): lax.psum_scatter(matmul_right_t(grad_qkv, projection).astype(low), 'seq',...  35.3 us
  transfers between devices with their start and end apart: 15, of which 12 were waited for; matrix products, arithmetic and copies ran while one was open for 26% of the time, Pallas kernels for 0%

profile of v1, /device:TPU:0, one launch (start us, length us, event | category | flops | bytes accessed | tf_op | source)
XLA Modules:
  0.0 941.2 jit_solution(15871986506294395785)
XLA Ops:
  12.9 43.4 %all-gather = bf16[32,32,8]{1,2,0:T(8,128)(2,1)S(1)} all-gather(bf16[1,32,8]{1,2,0:T(8,128)(2,1)S(1)} %bitcast.258), channel_id=1, replica_groups=mesh['shard'=8,'seq'=4] {'shard','seq'}, dimensions={0}, use_global_device_ids=true | all-gather | bytes 16896 | tf_op jit(solution)/shard_map/all_gather | solution.py:164
  57.1 2.4 fusion.40
  62.1 16.5 %all_to_all.45 = bf16[4,32,1792]{2,1,0:T(8,128)(2,1)} all-to-all(bf16[4,32,1792]{2,1,0:T(8,128)(2,1)S(1)} %pad_maximum_fusion.4), channel_id=1, replica_groups=mesh['shard'=8,'seq'=4] {'seq'}, dimensions={0} | all-to-all | bytes 917504 | tf_op jit(solution)/shard_map/all_to_all | solution.py:156
  79.5 10.0 %all-gather.9.cloned.1.call-done = bf16[1568,1024]{1,0:T(8,128)(2,1)} async-done(((bf16[392,1024]{1,0:T(8,128)(2,1)}), bf16[1568,1024]{1,0:T(8,128)(2,1)}) %all-gather.9.cloned.1.call-update) | async-done | bytes 3211280 | tf_op jit(solution)/shard_map/all_gather | solution.py:171
  89.6 64.7 %all-gather.11.cloned.1.call-done = bf16[1024,1792]{1,0:T(8,128)(2,1)} async-done(((bf16[128,1792]{1,0:T(8,128)(2,1)}), bf16[1024,1792]{1,0:T(8,128)(2,1)}) %all-gather.11.cloned.1.call-update) | async-done | bytes 3670032 | tf_op jit(solution)/shard_map/all_gather | solution.py:157
  154.3 5.0 add_convert_fusion.1
  163.0 8.5 multiply_reduce_fusion.2
  171.5 4.2 multiply_reduce_fusion.3
  175.7 16.2 %fusion.1 = f32[4,784]{1,0:T(4,128)S(1)} fusion(f32[4,784,1568]{2,1,0:T(8,128)} %get-tuple-element.61, f32[4,784]{1,0:T(4,128)S(1)} %get-tuple-element.60), kind=kLoop, calls=%fused_computation.11 | loop fusion | flops 14748608 | bytes 19694080 | tf_op jit(solution)/shard_map/reduce_sum | solution.py:71
  192.0 10.5 %fusion.63 = bf16[784,4,64]{0,2,1:T(8,128)(2,1)} fusion(bf16[1568,4,64]{0,2,1:T(8,128)(2,1)} %bitcast.205, f32[4,784,1568]{2,1,0:T(8,128)} %get-tuple-element.61, f32[4,784]{1,0:T(4,128)S(1)} %fusion.1, f32[4,784]{1,0:T(4,128)S(1)} %get-tuple-element.60), kind=kOutput, calls=%fused_computation.112 | convolution fusion | flops 649277440 | bytes 20898304 | tf_op jit(solution)/shard_map/hqk,khd->qhd/dot_general | solution.py:73
  202.5 4.1 fusion
  206.6 6.7 fusion.62
  214.7 1.6 all_to_all.33
  217.3 14.3 %all_to_all.46 = bf16[4,392,256]{2,1,0:T(8,128)(2,1)S(1)} all-to-all(bf16[4,392,256]{2,1,0:T(8,128)(2,1)S(1)} %copy.105), channel_id=1, replica_groups=mesh['shard'=8,'seq'=4] {'seq'}, dimensions={0} | all-to-all | bytes 1605632 | tf_op jit(solution)/shard_map/all_to_all | solution.py:177
  231.8 3.0 fusion.81
  236.4 1.8 convert_element_type.184
  238.9 1.7 convert_reduce_fusion.5
  240.7 18.0 %all-gather.1 = bf16[8,1,128]{2,1,0:T(2,128)(2,1)S(1)} all-gather(bf16[1,1,128]{2,1,0:T(2,128)(2,1)S(1)} %convert_bitcast_fusion.1), channel_id=1, replica_groups=mesh['shard'=8,'seq'=4] {'shard'}, dimensions={0}, use_global_device_ids=true | all-gather | bytes 2304 | tf_op jit(solution)/shard_map/all_gather | solution.py:166
  258.7 4.5 all-gather.15.cloned.1.call-done
  263.2 8.8 fusion.37
  272.0 42.8 %all-gather.17.cloned.1.call-done = bf16[1024,1024]{1,0:T(8,128)(2,1)} async-done(((bf16[128,1024]{1,0:T(8,128)(2,1)}), bf16[1024,1024]{1,0:T(8,128)(2,1)}) %all-gather.17.cloned.1.call-update) | async-done | bytes 2097168 | tf_op jit(solution)/shard_map/all_gather | solution.py:159
  314.9 29.4 %all-gather.19.cloned.1.call-done = bf16[1568,1024]{1,0:T(8,128)(2,1)} async-done(((bf16[392,1024]{1,0:T(8,128)(2,1)}), bf16[1568,1024]{1,0:T(8,128)(2,1)}) %all-gather.19.cloned.1.call-update) | async-done | bytes 3211280 | tf_op jit(solution)/shard_map/all_gather | solution.py:187
  344.3 22.9 %convert_reduce_fusion = (f32[1024]{0:T(1024)}, bf16[1568,1024]{1,0:T(8,128)(2,1)S(1)}, f32[1568,1024]{1,0:T(8,128)}) fusion(f32[1568,1024]{1,0:T(8,128)} %fusion.37, f32[1024]{0:T(1024)S(1)} %bitcast.256, bf16[1568,1024]{1,0:T(8,128)(2,1)} %all-gather.19.cloned.1.call-done, bf16[1024,1024]{1,0:T(8,128)(2,1)} %all-gather.17.cloned.1.call-done), kind=kOutput, calls=%fused_computation.22 | convolution fusion | flops 3408755712 | bytes 21372928 | tf_op jit(solution)/shard_map/dot_general | solution.py:21
  367.2 1.7 copy-done.42
  368.9 5.0 convolution_convert_fusion.1
  374.0 6.6 multiply_convert_fusion.2
  380.6 1.8 copy-done.20
  382.4 4.9 convolution_convert_fusion.2
  387.5 8.3 convolution_convert_fusion.4
  395.8 16.6 %reduce-scatter.14.cloned.1.call-done = bf16[392,1024]{1,0:T(8,128)(2,1)} async-done(((bf16[1568,1024]{1,0:T(8,128)(2,1)}), bf16[392,1024]{1,0:T(8,128)(2,1)}) %reduce-scatter.14.cloned.1.call-update) | async-done | bytes 802832 | tf_op jit(solution)/shard_map/reduce_scatter | solution.py:199
  412.4 1.9 fusion.52
  414.4 38.9 %reduce-scatter.12.cloned.1.call-done = bf16[392,1024]{1,0:T(8,128)(2,1)} async-done(((bf16[1568,1024]{1,0:T(8,128)(2,1)}), bf16[392,1024]{1,0:T(8,128)(2,1)}) %reduce-scatter.12.cloned.1.call-update) | async-done | bytes 802832 | tf_op jit(solution)/shard_map/reduce_scatter | solution.py:191
  453.3 3.5 convert_reduce_fusion.6
  458.8 4.2 all-to-all-start.2
  463.1 2.7 convolution_convert_fusion.3
  466.1 8.8 all-to-all-done.2
  478.0 13.8 %multiply_reduce_fusion.1 = (f32[4,784]{1,0:T(4,128)S(1)}, f32[4,784,1568]{2,1,0:T(8,128)}) fusion(f32[4,784,1568]{2,1,0:T(8,128)} %copy-done, f32[4,784]{1,0:T(4,128)S(1)} %log_add_fusion.1, bf16[784,4,64]{0,2,1:T(8,128)(2,1)S(1)} %slice.98, bf16[1568,4,64]{0,2,1:T(8,128)(2,1)S(1)} %bitcast.207), kind=kOutput, calls=%fused_computation.4 | convolution fusion | flops 649073600 | bytes 40567296 | tf_op jit(solution)/shard_map/qhd,khd->hqk/dot_general | solution.py:100
  491.9 14.5 %multiply_convert_fusion.1 = bf16[4,784,1568]{2,1,0:T(8,128)(2,1)S(1)} fusion(f32[4,784,1568]{2,1,0:T(8,128)} %get-tuple-element.67, f32[4,784,1568]{2,1,0:T(8,128)} %copy-done, f32[4,784]{1,0:T(4,128)S(1)} %get-tuple-element.66, f32[4,784]{1,0:T(4,128)S(1)} %log_add_fusion.1), kind=kLoop, calls=%fused_computation.3 | loop fusion | flops 24586240 | bytes 49197568 | tf_op jit(solution)/shard_map/convert_element_type | solution.py:104
  506.4 3.9 copy-done.1
  510.3 3.2 fusion.61
  513.6 13.5 %multiply_reduce_fusion = (f32[4,784]{1,0:T(4,128)S(1)}, f32[4,784,1568]{2,1,0:T(8,128)}) fusion(f32[4,784,1568]{2,1,0:T(8,128)} %get-tuple-element.61, f32[4,784]{1,0:T(4,128)S(1)} %log_add_fusion, bf16[784,4,64]{0,2,1:T(8,128)(2,1)S(1)} %slice.100, bf16[1568,4,64]{0,2,1:T(8,128)(2,1)S(1)} %bitcast.208), kind=kOutput, calls=%fused_computation.1 | convolution fusion | flops 649073600 | bytes 40567296 | tf_op jit(solution)/shard_map/qhd,khd->hqk/dot_general | solution.py:100
  527.0 14.7 %multiply_convert_fusion = bf16[4,784,1568]{2,1,0:T(8,128)(2,1)S(1)} fusion(f32[4,784,1568]{2,1,0:T(8,128)} %get-tuple-element.69, f32[4,784,1568]{2,1,0:T(8,128)} %get-tuple-element.61, f32[4,784]{1,0:T(4,128)S(1)} %get-tuple-element.68, f32[4,784]{1,0:T(4,128)S(1)} %log_add_fusion), kind=kLoop, calls=%fused_computation | loop fusion | flops 24586240 | bytes 49197568 | tf_op jit(solution)/shard_map/convert_element_type | solution.py:104
  541.8 4.0 fusion.60
  547.2 2.9 pad_maximum_fusion.3
  550.2 5.9 fusion.82
  556.1 6.9 fusion.23
  563.0 5.8 fusion.4
  568.7 11.3 %fusion.20 = bf16[4,64,1568]{2,1,0:T(8,128)(2,1)S(1)} fusion(f32[4,64,1568]{2,1,0:T(8,128)} %fusion.4, bf16[784,4,64]{0,2,1:T(8,128)(2,1)} %copy-done.10, f32[4,784,1568]{2,1,0:T(8,128)} %copy-done, f32[4,784]{1,0:T(4,128)S(1)} %log_add_fusion.1), kind=kOutput, calls=%fused_computation.47 | convolution fusion | flops 644962304 | bytes 22491392 | tf_op jit(solution)/shard_map/hqk,qhd->khd/dot_general | solution.py:117
  580.1 6.4 convolution_convert_fusion
  586.8 7.0 convolution_convert_fusion.5
  593.9 3.0 convolution_convert_fusion.6
  596.9 2.2 pad_maximum_fusion
  599.1 6.0 copy.117
  606.6 21.2 %all-reduce = f32[1024]{0:T(1024)S(1)} all-reduce(f32[1024]{0:T(1024)S(1)} %copy-done.35), channel_id=8, replica_groups=mesh['shard'=8,'seq'=4] {'shard'}, use_global_device_ids=true, to_apply=%region_28.0.clone | all-reduce | flops 1024 | bytes 8192
  628.4 1.8 convert_element_type.220
  630.1 1.8 convert_reduce_fusion.1
  632.1 33.0 %reduce-scatter.18.cloned.1.call-done = bf16[32,1024]{1,0:T(8,128)(2,1)} async-done(((bf16[1024,1024]{1,0:T(8,128)(2,1)}), bf16[32,1024]{1,0:T(8,128)(2,1)}) %reduce-scatter.18.cloned.1.call-update) | async-done | bytes 65552 | tf_op jit(solution)/shard_map/reduce_scatter | solution.py:243
  665.1 1.5 convert_element_type.217
  666.6 35.3 %reduce-scatter.16.cloned.1.call-done = bf16[392,1024]{1,0:T(8,128)(2,1)} async-done(((bf16[1568,1024]{1,0:T(8,128)(2,1)}), bf16[392,1024]{1,0:T(8,128)(2,1)}) %reduce-scatter.16.cloned.1.call-update) | async-done | bytes 802832 | tf_op jit(solution)/shard_map/reduce_scatter | solution.py:216
  701.9 2.0 fusion.53
  705.0 81.3 %reduce-scatter.24.cloned.1.call-done = bf16[128,1792]{1,0:T(8,128)(2,1)} async-done(((bf16[1024,1792]{1,0:T(8,128)(2,1)}), bf16[128,1792]{1,0:T(8,128)(2,1)}) %reduce-scatter.24.cloned.1.call-update) | async-done | bytes 458768 | tf_op jit(solution)/shard_map/reduce_scatter | solution.py:234
  786.3 3.5 all-to-all-start.3
  789.8 2.6 fusion.65
  792.4 131.9 %reduce-scatter.22.cloned.1.call-done = f32[32,8]{1,0:T(8,128)} async-done(((f32[1024,8]{1,0:T(8,128)}), f32[32,8]{1,0:T(8,128)}) %reduce-scatter.22.cloned.1.call-update) | async-done | bytes 1040
  (216 shorter events, 37.7 us)
Async XLA Ops:
  7.2 53.4 %copy-start.24 = (f32[32,1024]{1,0:T(8,128)S(1)}, f32[32,1024]{1,0:T(8,128)}, u32[]{:S(2)}) copy-start(f32[32,1024]{1,0:T(8,128)} %param.24) | copy-start | bytes 393220
  7.2 53.6 %copy-start.25 = (f32[32,1024]{1,0:T(8,128)S(1)}, f32[32,1024]{1,0:T(8,128)}, u32[]{:S(2)}) copy-start(f32[32,1024]{1,0:T(8,128)} %param.25) | copy-start | bytes 393220
  7.2 54.5 %copy-start.23 = (f32[32,4096]{1,0:T(8,128)S(1)}, f32[32,4096]{1,0:T(8,128)}, u32[]{:S(2)}) copy-start(f32[32,4096]{1,0:T(8,128)} %param.31) | copy-start | bytes 1572868
  7.2 82.4 %all-gather.9.cloned.1.call-start = ((), (), s32[]{:S(2)}) async-start(), calls=%async_computation.11 | async-start | bytes 4014080 | tf_op jit(solution)/shard_map/all_gather | solution.py:171
  8.7 52.2 %copy-start.29 = (f32[392]{0:T(512)}, f32[392]{0:T(512)S(1)}, u32[]{:S(2)}) copy-start(f32[392]{0:T(512)S(1)} %broadcast_multiply_fusion.5) | copy-start | bytes 4708
  10.2 50.7 %copy-start.31 = (f32[392]{0:T(512)}, f32[392]{0:T(512)S(1)}, u32[]{:S(2)}) copy-start(f32[392]{0:T(512)S(1)} %add_rsqrt_fusion.1) | copy-start | bytes 4708
  56.4 22.4 %copy-start.26 = (f32[32,1024]{1,0:T(8,128)S(1)}, f32[32,1024]{1,0:T(8,128)}, u32[]{:S(2)}) copy-start(f32[32,1024]{1,0:T(8,128)} %param.27) | copy-start | bytes 393220
  57.1 3.8 copy-start.27
  59.5 94.8 %all-gather.11.cloned.1.call-start = ((), (), s32[]{:S(2)}) async-start(), calls=%async_computation.12 | async-start | bytes 4128768 | tf_op jit(solution)/shard_map/all_gather | solution.py:157
  78.7 153.1 %all-gather.13.cloned.1.call-start = ((), (), s32[]{:S(2)}) async-start(), calls=%async_computation.13 | async-start | bytes 2162688 | tf_op jit(solution)/shard_map/all_gather | solution.py:160
  79.4 183.8 %all-gather.15.cloned.1.call-start = ((), (), s32[]{:S(2)}) async-start(), calls=%async_computation.14 | async-start | bytes 4014080 | tf_op jit(solution)/shard_map/all_gather | solution.py:181
  160.4 11.2 %copy-start.3 = (bf16[1568,256]{0,1:T(8,128)(2,1)}, bf16[1568,256]{0,1:T(8,128)(2,1)S(1)}, u32[]{:S(2)}) copy-start(bf16[1568,256]{0,1:T(8,128)(2,1)S(1)} %copy.103) | copy-start | bytes 2408452
  161.7 9.9 %copy-start.14 = (bf16[784,256]{0,1:T(8,128)(2,1)}, bf16[784,256]{0,1:T(8,128)(2,1)S(1)}, u32[]{:S(2)}) copy-start(bf16[784,256]{0,1:T(8,128)(2,1)S(1)} %copy.104) | copy-start | bytes 1204228
  163.0 8.5 copy-start.12
  175.7 30.8 %copy-start = (f32[4,784,1568]{2,1,0:T(8,128)}, f32[4,784,1568]{2,1,0:T(8,128)S(1)}, u32[]{:S(2)}) copy-start(f32[4,784,1568]{2,1,0:T(8,128)S(1)} %get-tuple-element.63) | copy-start | bytes 59006980
  213.2 18.5 %copy-start.5 = (bf16[1,392,1024]{2,1,0:T(8,128)(2,1)S(1)}, bf16[1,392,1024]{2,1,0:T(8,128)(2,1)}, u32[]{:S(2)}) copy-start(bf16[1,392,1024]{2,1,0:T(8,128)(2,1)} %param.18) | copy-start | bytes 2408452
  231.8 3.4 copy-start.21
  234.8 4.1 copy-start.19
  234.8 5.9 copy-start.40
  236.4 78.5 %all-gather.17.cloned.1.call-start = ((), (), s32[]{:S(2)}) async-start(), calls=%async_computation.15 | async-start | bytes 2359296 | tf_op jit(solution)/shard_map/all_gather | solution.py:159
  238.2 106.1 %all-gather.19.cloned.1.call-start = ((), (), s32[]{:S(2)}) async-start(), calls=%async_computation.17 | async-start | bytes 4014080 | tf_op jit(solution)/shard_map/all_gather | solution.py:187
  240.7 171.8 %reduce-scatter.14.cloned.1.call-start = ((), (), s32[]{:S(2)}) async-start(), calls=%async_computation.18 | async-start | bytes 4014080 | tf_op jit(solution)/shard_map/reduce_scatter | solution.py:199
  344.3 24.6 %copy-start.36 = (bf16[1024,1792]{1,0:T(8,128)(2,1)S(1)}, bf16[1024,1792]{1,0:T(8,128)(2,1)}, u32[]{:S(2)}) copy-start(bf16[1024,1792]{1,0:T(8,128)(2,1)} %all-gather.11.cloned.1.call-done) | copy-start | bytes 11010052
  367.2 1.7 copy-start.42
  373.9 79.3 %reduce-scatter.12.cloned.1.call-start = ((), (), s32[]{:S(2)}) async-start(), calls=%async_computation.16 | async-start | bytes 4014080 | tf_op jit(solution)/shard_map/reduce_scatter | solution.py:191
  374.0 8.4 copy-start.39
  380.6 1.8 copy-start.20
  387.3 66.0 %copy-start.34 = (f32[1,1024]{1,0:T(1,128)S(1)}, f32[1,1024]{1,0:T(1,128)}, u32[]{:S(2)}) copy-start(f32[1,1024]{1,0:T(1,128)} %get-tuple-element.42) | copy-start | bytes 12292
  387.3 241.0 %reduce-scatter.20.cloned.1.call-start = ((), (), s32[]{:S(2)}) async-start(), calls=%async_computation.21 | async-start | bytes 2359296 | tf_op jit(solution)/shard_map/reduce_scatter | solution.py:240
  453.3 3.5 copy-start.38
  456.8 9.0 copy-start.8
  456.8 6.3 copy-start.22
  458.8 16.1 %all-to-all-start.2 = ((bf16[392,4,256]{2,0,1:T(8,128)(2,1)}), bf16[392,4,256]{2,0,1:T(8,128)(2,1)}, u32[]{:S(2)}, u32[]{:S(2)}) async-start(bf16[392,4,256]{2,0,1:T(8,128)(2,1)} %bitcast.196), calls=%async_computation.4 | async-start | bytes 1605632 | tf_op jit(solution)/shard_map/all_to_all | solution.py:210
  463.0 202.0 %reduce-scatter.18.cloned.1.call-start = ((), (), s32[]{:S(2)}) async-start(), calls=%async_computation.20 | async-start | bytes 2162688 | tf_op jit(solution)/shard_map/reduce_scatter | solution.py:243
  465.8 12.2 %copy-start.7 = (bf16[1568,256]{0,1:T(8,128)(2,1)S(1)}, bf16[1568,256]{0,1:T(8,128)(2,1)}, u32[]{:S(2)}) copy-start(bf16[1568,256]{0,1:T(8,128)(2,1)} %copy.101) | copy-start | bytes 2408452
  465.8 236.0 %reduce-scatter.16.cloned.1.call-start = ((), (), s32[]{:S(2)}) async-start(), calls=%async_computation.19 | async-start | bytes 4014080 | tf_op jit(solution)/shard_map/reduce_scatter | solution.py:216
  477.0 14.8 %copy-start.10 = (bf16[784,4,64]{0,2,1:T(8,128)(2,1)}, bf16[784,4,64]{0,2,1:T(8,128)(2,1)S(1)}, u32[]{:S(2)}) copy-start(bf16[784,4,64]{0,2,1:T(8,128)(2,1)S(1)} %slice.98) | copy-start | bytes 1204228
  478.0 35.5 %copy-start.11 = (bf16[784,4,64]{0,2,1:T(8,128)(2,1)}, bf16[784,4,64]{0,2,1:T(8,128)(2,1)S(1)}, u32[]{:S(2)}) copy-start(bf16[784,4,64]{0,2,1:T(8,128)(2,1)S(1)} %slice.100) | copy-start | bytes 1204228
  491.8 18.5 %copy-start.4 = (bf16[1568,256]{0,1:T(8,128)(2,1)S(1)}, bf16[1568,256]{0,1:T(8,128)(2,1)}, u32[]{:S(2)}) copy-start(bf16[1568,256]{0,1:T(8,128)(2,1)} %copy-done.3) | copy-start | bytes 2408452
  506.4 3.9 copy-start.1
  541.7 5.5 copy-start.2
  541.7 8.4 copy-start.13
  541.8 21.2 %slice-start = ((s8[20873216]{0:T(1024)(128)(4,1)}), s8[4194304]{0:T(1024)(128)(4,1)S(1)}, s32[]{:S(2)}) async-start(s8[20873216]{0:T(1024)(128)(4,1)} %bitcast.199), calls=%async_computation.24 | async-start | bytes 8388608
  541.8 21.2 %slice-start.1 = ((s8[20873216]{0:T(1024)(128)(4,1)}), s8[4194304]{0:T(1024)(128)(4,1)S(1)}, s32[]{:S(2)}) async-start(s8[20873216]{0:T(1024)(128)(4,1)} %bitcast.199), calls=%async_computation.25 | async-start | bytes 8388608
  550.2 5.9 copy-start.15
  550.2 12.8 %slice-start.2 = ((s8[20873216]{0:T(1024)(128)(4,1)}), s8[4194304]{0:T(1024)(128)(4,1)S(1)}, s32[]{:S(2)}) async-start(s8[20873216]{0:T(1024)(128)(4,1)} %bitcast.199), calls=%async_computation.26 | async-start | bytes 8388608
  550.2 12.8 %slice-start.3 = ((s8[20873216]{0:T(1024)(128)(4,1)}), s8[4194304]{0:T(1024)(128)(4,1)S(1)}, s32[]{:S(2)}) async-start(s8[20873216]{0:T(1024)(128)(4,1)} %bitcast.199), calls=%async_computation.27 | async-start | bytes 8388608
  556.0 6.9 slice-start.4
  568.7 11.3 %copy-start.16 = (bf16[4,64,1568]{2,1,0:T(8,128)(2,1)S(1)}, bf16[4,64,1568]{2,1,0:T(8,128)(2,1)}, u32[]{:S(2)}) copy-start(bf16[4,64,1568]{2,1,0:T(8,128)(2,1)} %fusion.23) | copy-start | bytes 2408452
  568.7 11.4 %copy-start.17 = (bf16[1568,4,64]{0,2,1:T(8,128)(2,1)S(1)}, bf16[1568,4,64]{0,2,1:T(8,128)(2,1)}, u32[]{:S(2)}) copy-start(bf16[1568,4,64]{0,2,1:T(8,128)(2,1)} %pad_maximum_fusion.3) | copy-start | bytes 2408452
  580.1 13.8 %copy-start.18 = (bf16[4,64,1568]{2,1,0:T(8,128)(2,1)}, bf16[4,64,1568]{2,1,0:T(8,128)(2,1)S(1)}, u32[]{:S(2)}) copy-start(bf16[4,64,1568]{2,1,0:T(8,128)(2,1)S(1)} %fusion.20) | copy-start | bytes 2408452
  586.6 199.7 %reduce-scatter.24.cloned.1.call-start = ((), (), s32[]{:S(2)}) async-start(), calls=%async_computation.23 | async-start | bytes 4128768 | tf_op jit(solution)/shard_map/reduce_scatter | solution.py:234
  586.8 7.1 copy-start.37
  599.1 6.1 copy-start.41
  599.1 7.5 copy-start.35
  605.1 96.7 %copy-start.6 = (bf16[1,392,1024]{2,1,0:T(8,128)(2,1)S(1)}, bf16[1,392,1024]{2,1,0:T(8,128)(2,1)}, u32[]{:S(2)}) copy-start(bf16[1,392,1024]{2,1,0:T(8,128)(2,1)} %param.18) | copy-start | bytes 2408452
  605.1 96.7 %copy-start.28 = (f32[1,1024]{1,0:T(1,128)S(1)}, f32[1,1024]{1,0:T(1,128)}, u32[]{:S(2)}) copy-start(f32[1,1024]{1,0:T(1,128)} %copy-done.27) | copy-start | bytes 12292
  605.1 96.7 %copy-start.30 = (f32[392]{0:T(512)S(1)}, f32[392]{0:T(512)}, u32[]{:S(2)}) copy-start(f32[392]{0:T(512)} %copy-done.29) | copy-start | bytes 4708
  605.1 96.7 %copy-start.32 = (f32[392]{0:T(512)S(1)}, f32[392]{0:T(512)}, u32[]{:S(2)}) copy-start(f32[392]{0:T(512)} %copy-done.31) | copy-start | bytes 4708
  605.1 98.7 %copy-start.33 = (f32[1024]{0:T(1024)S(1)}, f32[1024]{0:T(1024)}, u32[]{:S(2)}) copy-start(f32[1024]{0:T(1024)} %get-tuple-element.28) | copy-start | bytes 12292
  605.2 184.6 %copy-start.9 = (f32[392,1024]{1,0:T(8,128)S(1)}, f32[392,1024]{1,0:T(8,128)}, u32[]{:S(2)}) copy-start(f32[392,1024]{1,0:T(8,128)} %copy-done.8) | copy-start | bytes 4816900
  605.2 319.1 %reduce-scatter.22.cloned.1.call-start = ((), (), s32[]{:S(2)}) async-start(), calls=%async_computation.22 | async-start | bytes 540672
  786.3 143.8 %all-to-all-start.3 = ((bf16[4,32,1792]{2,1,0:T(8,128)(2,1)}), bf16[4,32,1792]{2,1,0:T(8,128)(2,1)S(1)}, u32[]{:S(2)}, u32[]{:S(2)}) async-start(bf16[4,32,1792]{2,1,0:T(8,128)(2,1)} %bitcast.236), calls=%async_computation.6 | async-start | bytes 917504 | tf_op jit(solution)/shard_map/all_to_all | solution.py:235
Sparse Core Ops, SparseCore 0:
  59.6 29.8 all-gather.8
  91.8 62.4 all-gather.10
  157.7 54.9 all-gather.12
  236.5 26.6 all-gather.14
  265.8 49.0 all-gather.16
  316.9 27.4 all-gather.18
  374.1 38.2 reduce-scatter.13
  415.0 38.2 reduce-scatter.11
  456.8 68.3 reduce-scatter.19
  527.3 137.7 reduce-scatter.17
  667.6 34.1 reduce-scatter.15
  705.3 80.8 reduce-scatter.23
  789.1 135.1 reduce-scatter.21
